TPU v7x, 128 devices: a whole 4x4x4 slice. The times are simulated.
128 devices in a mesh: row: 16 (over y, z_hi, core), col: 8 (over x, z_lo).
Axes of the slice: x: 4, y: 4, z: 4 (z_hi: 2, z_lo: 2; z = z_hi * 2 + z_lo), core: 2. Of those that a mesh axis runs over, the one named last changes fastest.
Arguments:
- tokens: bfloat16 [6144, 4096], P('row', 'col'), may hold values from -6 to 6
- cotangent: bfloat16 [6144, 4096], P('row', 'col'), may hold values from -6 to 6
- gate_blocks: bfloat16 [32, 32, 128, 128], P('row', 'col'), may hold values from -0.1875 to 0.1875
- up_blocks: bfloat16 [32, 32, 128, 128], P('row', 'col'), may hold values from -0.1875 to 0.1875
- down_blocks: bfloat16 [32, 32, 128, 128], P('row', 'col'), may hold values from -0.09375 to 0.09375
- gate_cols: int32 [32, 32], P('row', 'col'), may hold values from 0 to 127, as said below
- up_cols: int32 [32, 32], P('row', 'col'), may hold values from 0 to 127, as said below
- down_cols: int32 [32, 32], P('row', 'col'), may hold values from 0 to 127, as said below
Outputs:
- output: bfloat16 [6144, 4096], P('row', 'col')
- tokens_grad: bfloat16 [6144, 4096], P('row', 'col')
- gate_grad: bfloat16 [32, 32, 128, 128], P('row', 'col')
- up_grad: bfloat16 [32, 32, 128, 128], P('row', 'col')
- down_grad: bfloat16 [32, 32, 128, 128], P('row', 'col')
Inputs may be any that keep to these rules, and one draw needn't show every extreme that they name: In every block row of gate_cols, slots c * 4 to c * 4 + 3 hold 4 different block columns, all in c * 16 to c * 16 + 15. In every block row of up_cols, slots c * 4 to c * 4 + 3 hold 4 different block columns, all in c * 16 to c * 16 + 15. In every block row of down_cols, slots c * 4 to c * 4 + 3 hold 4 different block columns, all in c * 16 to c * 16 + 15.
All inputs are finite; a program needn't handle non-finite values.
Results may differ from a plain program's by a relative error of at most 0.022.
Values may be sent and summed in bfloat16 or wider, within the bound.
No kernel may reach another device: no remote copies, remote signals or barrier semaphores. Data moves between devices by JAX's collectives and lax.ppermute only.
A program may use at most 256 MiB of HBM per device.

v0:
```python
import jax
import jax.numpy as jnp
from jax import lax
from jax.sharding import PartitionSpec as P


def spread_columns(products, columns, local_width):
    tok_rows = products.shape[0]
    flat = products.reshape(tok_rows, -1, products.shape[3])
    empty = jnp.zeros((tok_rows, local_width, products.shape[3]), jnp.float32)
    return empty.at[:, columns.reshape(-1)].add(flat)


def body(tokens, cotangent, gate_blocks, up_blocks, down_blocks, gate_cols, up_cols, down_cols):
    local_rows = gate_blocks.shape[0]
    local_slots = gate_blocks.shape[1]
    block_size = gate_blocks.shape[2]
    local_width = 4 * local_slots
    offset = lax.axis_index("col") * local_width
    tok_rows = tokens.shape[0]
    features, cot_features = (
        lax.all_gather(tokens, "col", axis=1, tiled=True),
        lax.all_gather(cotangent, "col", axis=1, tiled=True),
    )
    blocks_all = features.shape[1] // block_size
    feature_blocks = features.reshape(tok_rows, blocks_all, block_size)
    cotangent_blocks = cot_features.reshape(tok_rows, blocks_all, block_size)
    gate_vals = lax.all_gather(gate_blocks, "row", axis=0, tiled=True)
    up_vals = lax.all_gather(up_blocks, "row", axis=0, tiled=True)
    gate_piece = lax.all_gather(gate_cols.astype(jnp.bfloat16), "row", axis=0, tiled=True)
    up_piece = lax.all_gather(up_cols.astype(jnp.bfloat16), "row", axis=0, tiled=True)
    inputs = feature_blocks
    gate_local = gate_piece.astype(jnp.int32) - offset
    up_local = up_piece.astype(jnp.int32) - offset
    gate_products = jnp.einsum(
        "tkd,kjde->tkje", inputs, gate_vals, preferred_element_type=jnp.float32
    )
    up_products = jnp.einsum("tkd,kjde->tkje", inputs, up_vals, preferred_element_type=jnp.float32)
    gate_acc = spread_columns(gate_products, gate_local, local_width)
    up_acc = spread_columns(up_products, up_local, local_width)
    gate_gate_idx = gate_local
    gate_up_idx = up_local
    gate_acc, up_acc, gate_idx, up_idx = (gate_acc, up_acc, gate_gate_idx, gate_up_idx)
    silu_gate = jax.nn.silu(gate_acc)
    hidden_blocks = (silu_gate * up_acc).astype(jnp.bfloat16)
    down_vals = lax.all_gather(down_blocks, "row", axis=0, tiled=True)
    down_piece = lax.all_gather(down_cols.astype(jnp.bfloat16), "row", axis=0, tiled=True)
    down_local = down_piece.astype(jnp.int32) - offset
    chosen = jnp.take(hidden_blocks, down_local, axis=1)
    partial_value = jnp.einsum(
        "tkje,kjde->tkd", chosen, down_vals, preferred_element_type=jnp.float32
    )
    out_acc = partial_value
    down_down_idx = down_local
    out_acc, down_idx = (out_acc, down_down_idx)
    output = lax.psum_scatter(
        out_acc.reshape(tok_rows, -1).astype(jnp.bfloat16), "col", scatter_dimension=1, tiled=True
    )
    inputs = cotangent_blocks
    products = jnp.einsum(
        "tkd,kjde->tkje",
        inputs,
        lax.all_gather(down_blocks, "row", axis=0, tiled=True),
        preferred_element_type=jnp.float32,
    )
    hidden_grad = spread_columns(products, down_idx, local_width)
    sigmoid_gate = jax.nn.sigmoid(gate_acc)
    up_delta = (hidden_grad * silu_gate).astype(jnp.bfloat16)
    gate_delta = (
        hidden_grad * up_acc * sigmoid_gate * (1.0 + gate_acc * (1.0 - sigmoid_gate))
    ).astype(jnp.bfloat16)
    gate_vals = lax.all_gather(gate_blocks, "row", axis=0, tiled=True)
    up_vals = lax.all_gather(up_blocks, "row", axis=0, tiled=True)
    gate_local = gate_idx
    up_local = up_idx
    partial_value = jnp.einsum(
        "tkje,kjde->tkd",
        jnp.take(gate_delta, gate_local, axis=1),
        gate_vals,
        preferred_element_type=jnp.float32,
    )
    partial_value = partial_value + jnp.einsum(
        "tkje,kjde->tkd",
        jnp.take(up_delta, up_local, axis=1),
        up_vals,
        preferred_element_type=jnp.float32,
    )
    tokens_grad = lax.psum_scatter(
        partial_value.reshape(tok_rows, -1).astype(jnp.bfloat16),
        "col",
        scatter_dimension=1,
        tiled=True,
    )
    grad_scale = float(tok_rows * lax.axis_size("row")) ** (-0.5)
    groups = local_rows * lax.axis_size("row") // local_rows

    def one_group(group_index):
        group_first = group_index * local_rows
        inputs = lax.dynamic_slice_in_dim(feature_blocks, group_first, local_rows, 1)
        cot_inputs = lax.dynamic_slice_in_dim(cotangent_blocks, group_first, local_rows, 1)
        gate_local = lax.dynamic_slice_in_dim(gate_idx, group_first, local_rows, 0)
        up_local = lax.dynamic_slice_in_dim(up_idx, group_first, local_rows, 0)
        down_local = lax.dynamic_slice_in_dim(down_idx, group_first, local_rows, 0)
        gate_term = jnp.einsum(
            "tkd,tkje->kjde",
            inputs,
            jnp.take(gate_delta, gate_local, axis=1),
            preferred_element_type=jnp.float32,
        )
        up_term = jnp.einsum(
            "tkd,tkje->kjde",
            inputs,
            jnp.take(up_delta, up_local, axis=1),
            preferred_element_type=jnp.float32,
        )
        down_term = jnp.einsum(
            "tkd,tkje->kjde",
            cot_inputs,
            jnp.take(hidden_blocks, down_local, axis=1),
            preferred_element_type=jnp.float32,
        )
        return jnp.stack([gate_term, up_term, down_term], axis=1) * grad_scale

    stacked = lax.map(one_group, jnp.arange(groups, dtype=jnp.int32))
    weight_grads = lax.psum_scatter(
        stacked.reshape((local_rows * lax.axis_size("row"),) + stacked.shape[2:]).astype(
            jnp.bfloat16
        ),
        "row",
        scatter_dimension=0,
        tiled=True,
    ).astype(jnp.float32)
    gate_grad = weight_grads[:, 0].astype(jnp.bfloat16)
    up_grad = weight_grads[:, 1].astype(jnp.bfloat16)
    down_grad = weight_grads[:, 2].astype(jnp.bfloat16)
    return (output, tokens_grad, gate_grad, up_grad, down_grad)


def solution(mesh):
    in_specs = (
        P("row", "col"),
        P("row", "col"),
        P("row", "col", None, None),
        P("row", "col", None, None),
        P("row", "col", None, None),
        P("row", "col"),
        P("row", "col"),
        P("row", "col"),
    )
    out_specs = (
        P("row", "col"),
        P("row", "col"),
        P("row", "col", None, None),
        P("row", "col", None, None),
        P("row", "col", None, None),
    )
    return jax.shard_map(body, mesh=mesh, in_specs=in_specs, out_specs=out_specs, check_vma=False)
```

profile of v0, /device:TPU:2, one launch (start us, length us, event | category | flops | bytes accessed | tf_op | source)
XLA Modules:
  0.0 1250.2 jit_solution(13534747205828137103)
XLA Ops:
  14.0 28.0 %all-gather = bf16[16,2,4]{2,1,0:T(2,128)(2,1)S(1)} all-gather(bf16[1,2,4]{2,1,0:T(2,128)(2,1)S(1)} %convert_bitcast_fusion.2), channel_id=1, replica_groups=mesh['row'=16,'col'=8] {'row'}, dimensions={0}, use_global_device_ids=true | all-gather | bytes 272 | tf_op jit(solution)/shard_map/all_gather | solution.py:30
  42.8 19.2 %all-gather.1 = bf16[16,2,4]{2,1,0:T(2,128)(2,1)S(1)} all-gather(bf16[1,2,4]{2,1,0:T(2,128)(2,1)S(1)} %convert_bitcast_fusion.1), channel_id=1, replica_groups=mesh['row'=16,'col'=8] {'row'}, dimensions={0}, use_global_device_ids=true | all-gather | bytes 272 | tf_op jit(solution)/shard_map/all_gather | solution.py:31
  62.8 24.5 %all-gather.2 = bf16[16,2,4]{2,1,0:T(2,128)(2,1)S(1)} all-gather(bf16[1,2,4]{2,1,0:T(2,128)(2,1)S(1)} %convert_bitcast_fusion), channel_id=1, replica_groups=mesh['row'=16,'col'=8] {'row'}, dimensions={0}, use_global_device_ids=true | all-gather | bytes 272 | tf_op jit(solution)/shard_map/all_gather | solution.py:47
  87.4 55.0 %all-gather.9.cloned.1.call-done = bf16[32,4,128,128]{3,2,1,0:T(8,128)(2,1)} async-done(((bf16[2,4,128,128]{3,2,1,0:T(8,128)(2,1)}), bf16[32,4,128,128]{3,2,1,0:T(8,128)(2,1)}) %all-gather.9.cloned.1.call-update) | async-done | bytes 4194320 | tf_op jit(solution)/shard_map/all_gather | solution.py:28
  142.5 15.2 %fusion.52 = f32[32,4,128,384]{3,2,1,0:T(8,128)} fusion(bf16[32,4,128,128]{3,2,1,0:T(8,128)(2,1)} %all-gather.9.cloned.1.call-done, bf16[384,32,128,1]{0,2,3,1:T(8,128)(2,1)} %bitcast.176), kind=kOutput, calls=%fused_computation.100 | convolution fusion | flops 1610612736 | bytes 32505856 | tf_op jit(solution)/shard_map/tkd,kjde->tkje/dot_general | solution.py:35
  157.7 25.0 %copy.57 = f32[384,128,128]{2,0,1:T(8,128)} copy(f32[384,128,128]{0,2,1:T(8,128)} %bitcast.166) | data formatting | bytes 50331648 | tf_op jit(solution)/shard_map/reshape | solution.py:9
  182.7 16.9 %all-gather.13.cloned.1.call-done = bf16[32,4,128,128]{3,2,1,0:T(8,128)(2,1)} async-done(((bf16[2,4,128,128]{3,2,1,0:T(8,128)(2,1)}), bf16[32,4,128,128]{3,2,1,0:T(8,128)(2,1)}) %all-gather.13.cloned.1.call-update) | async-done | bytes 4194320 | tf_op jit(solution)/shard_map/all_gather | solution.py:29
  199.6 14.1 %fusion.53 = f32[32,4,128,384]{3,2,1,0:T(8,128)} fusion(bf16[32,4,128,128]{3,2,1,0:T(8,128)(2,1)} %all-gather.13.cloned.1.call-done, bf16[384,32,128,1]{0,2,3,1:T(8,128)(2,1)S(1)} %bitcast.178), kind=kOutput, calls=%fused_computation.101 | convolution fusion | flops 1610612736 | bytes 32505856 | tf_op jit(solution)/shard_map/tkd,kjde->tkje/dot_general | solution.py:38
  213.7 24.8 %copy.60 = f32[384,128,128]{2,0,1:T(8,128)} copy(f32[384,128,128]{0,2,1:T(8,128)} %bitcast.167) | data formatting | bytes 50331648 | tf_op jit(solution)/shard_map/reshape | solution.py:9
  238.5 32.8 %all-gather.17.cloned.1.call-done = bf16[384,4096]{0,1:T(8,128)(2,1)} async-done(((bf16[384,512]{0,1:T(8,128)(2,1)}), bf16[384,4096]{0,1:T(8,128)(2,1)}) %all-gather.17.cloned.1.call-update) | async-done | bytes 3145744 | tf_op jit(solution)/shard_map/all_gather | solution.py:23
  271.3 58.6 %all-gather.15.cloned.1.call-done = bf16[32,4,128,128]{3,2,1,0:T(8,128)(2,1)} async-done(((bf16[2,4,128,128]{3,2,1,0:T(8,128)(2,1)}), bf16[32,4,128,128]{3,2,1,0:T(8,128)(2,1)}) %all-gather.15.cloned.1.call-update) | async-done | bytes 4194320 | tf_op jit(solution)/shard_map/all_gather | solution.py:46
  329.9 14.9 %fusion.54 = f32[32,4,128,384]{3,2,1,0:T(8,128)} fusion(bf16[32,4,128,128]{3,2,1,0:T(8,128)(2,1)} %all-gather.15.cloned.1.call-done, bf16[384,32,128,1]{0,2,3,1:T(8,128)(2,1)} %bitcast.182), kind=kOutput, calls=%fused_computation.102 | convolution fusion | flops 1610612736 | bytes 32505856 | tf_op jit(solution)/shard_map/tkd,kjde->tkje/dot_general | solution.py:60
  344.9 24.7 %copy.65 = f32[384,128,128]{2,0,1:T(8,128)} copy(f32[384,128,128]{0,2,1:T(8,128)} %bitcast.168) | data formatting | bytes 50331648 | tf_op jit(solution)/shard_map/reshape | solution.py:9
  369.8 38.7 %scatter_fusion = f32[384,16,128]{2,0,1:T(8,128)S(1)} fusion(f32[384,16,128]{2,0,1:T(8,128)S(1)} %broadcast.80.clone, s32[128]{0:T(128)S(1)} %fusion.46, f32[128,384,128]{2,1,0:T(8,128)} %bitcast.169), kind=kCustom, calls=%fused_computation.6 | custom fusion | flops 6291456 | bytes 75497984 | tf_op jit(solution)/shard_map/scatter-add | solution.py:11
  410.8 63.0 %scatter_fusion.1 = f32[384,16,128]{2,0,1:T(8,128)} fusion(f32[384,16,128]{2,0,1:T(8,128)} %broadcast.80.clone.2, s32[128]{0:T(128)S(1)} %fusion.47, f32[128,384,128]{2,1,0:T(8,128)} %bitcast.170), kind=kCustom, calls=%fused_computation.7 | custom fusion | flops 6291456 | bytes 75497984 | tf_op jit(solution)/shard_map/scatter-add | solution.py:11
  474.2 38.7 %scatter_fusion.2 = f32[384,16,128]{2,0,1:T(8,128)S(1)} fusion(f32[384,16,128]{2,0,1:T(8,128)S(1)} %broadcast.80.clone.1, s32[128]{0:T(128)S(1)} %fusion.48, f32[128,384,128]{2,1,0:T(8,128)} %bitcast.171), kind=kCustom, calls=%fused_computation.8 | custom fusion | flops 6291456 | bytes 75497984 | tf_op jit(solution)/shard_map/scatter-add | solution.py:11
  518.7 278.2 %while.10 = (s32[]{:T(128)}, bf16[16,2,3,4,128,128]{4,5,3,1,2,0:T(8,128)(2,1)}, s32[16]{0:T(128)S(1)}, s32[32,4]{1,0:T(8,128)S(1)}, bf16[384,16,128]{2,0,1:T(8,1...) while((s32[]{:T(128)}, ...), condition=%wide.region_6.9_spmd, body=%wide.region_5.8_spmd.sunk | while | flops 304352384 | bytes 31798688 | solution.py:124
  796.9 16.6 %copy.69 = bf16[16,2,3,4,128,128]{5,4,3,1,0,2:T(8,128)(2,1)} copy(bf16[16,2,3,4,128,128]{4,5,3,1,2,0:T(8,128)(2,1)} %get-tuple-element.64) | data formatting | bytes 25165824 | tf_op jit(solution)/shard_map/convert_element_type | solution.py:126
  814.9 8.5 gather_fusion.5
  823.4 8.6 gather_fusion.4
  853.4 8.8 gather_fusion.3
  874.5 217.0 %all-reduce.3.cloned.1.call-done = bf16[32,3,4,128,128]{4,3,2,0,1:T(8,128)(2,1)} async-done(((bf16[32,3,4,128,128]{4,3,2,0,1:T(8,128)(2,1)}), bf16[32,3,4,128,128]{4,3,2,0,1:T(8,128)(2,1)}) %all-reduce.3.cloned.1.call-update) | async-done | bytes 12582928
  1093.6 75.2 %reduce-scatter.8.cloned.1.call-done = bf16[384,512]{1,0:T(8,128)(2,1)} async-done(((bf16[384,4096]{1,0:T(8,128)(2,1)}), bf16[384,512]{1,0:T(8,128)(2,1)}) %reduce-scatter.8.cloned.1.call-update) | async-done | bytes 393232 | tf_op jit(solution)/shard_map/reduce_scatter | solution.py:88
  1168.8 74.5 %reduce-scatter.6.cloned.1.call-done = bf16[384,512]{1,0:T(8,128)(2,1)} async-done(((bf16[384,4096]{1,0:T(8,128)(2,1)}), bf16[384,512]{1,0:T(8,128)(2,1)}) %reduce-scatter.6.cloned.1.call-update) | async-done | bytes 393232 | tf_op jit(solution)/shard_map/reduce_scatter | solution.py:56
  (482 shorter events, 320.1 us)
Async XLA Ops:
  7.2 80.3 %all-gather.11.cloned.1.call-start = ((), (), s32[]{:S(2)}) async-start(), calls=%async_computation.3 | async-start | bytes 3538944 | tf_op jit(solution)/shard_map/all_gather | solution.py:22
  9.1 133.3 %all-gather.9.cloned.1.call-start = ((), (), s32[]{:S(2)}) async-start(), calls=%async_computation.2 | async-start | bytes 4456448 | tf_op jit(solution)/shard_map/all_gather | solution.py:28
  9.9 189.7 %all-gather.13.cloned.1.call-start = ((), (), s32[]{:S(2)}) async-start(), calls=%async_computation.4 | async-start | bytes 4456448 | tf_op jit(solution)/shard_map/all_gather | solution.py:29
  10.6 260.7 %all-gather.17.cloned.1.call-start = ((), (), s32[]{:S(2)}) async-start(), calls=%async_computation.7 | async-start | bytes 3538944 | tf_op jit(solution)/shard_map/all_gather | solution.py:23
  12.6 317.3 %all-gather.15.cloned.1.call-start = ((), (), s32[]{:S(2)}) async-start(), calls=%async_computation.5 | async-start | bytes 4456448 | tf_op jit(solution)/shard_map/all_gather | solution.py:46
  13.2 1078.4 %all-reduce.3.cloned.1.call-start = ((), (), s32[]{:S(2)}) async-start(), calls=%async_computation.9 | async-start | bytes 25165824
  42.0 45.3 %copy-start.11 = (s32[4,8,4]{2,1,0:T(8,128)}, s32[4,8,4]{2,1,0:T(8,128)S(1)}, u32[]{:S(2)}) copy-start(s32[4,8,4]{2,1,0:T(8,128)S(1)} %convert_subtract_fusion.2) | copy-start | bytes 1540
  62.0 95.7 %copy-start.13 = (s32[4,8,4]{2,1,0:T(8,128)}, s32[4,8,4]{2,1,0:T(8,128)S(1)}, u32[]{:S(2)}) copy-start(s32[4,8,4]{2,1,0:T(8,128)S(1)} %convert_subtract_fusion.1) | copy-start | bytes 1540
  87.2 70.4 %copy-start.9 = (s32[4,8,4]{2,1,0:T(8,128)}, s32[4,8,4]{2,1,0:T(8,128)S(1)}, u32[]{:S(2)}) copy-start(s32[4,8,4]{2,1,0:T(8,128)S(1)} %convert_subtract_fusion) | copy-start | bytes 1540
  157.7 41.9 %copy-start.6 = (bf16[384,4096]{0,1:T(8,128)(2,1)S(1)}, bf16[384,4096]{0,1:T(8,128)(2,1)}, u32[]{:S(2)}) copy-start(bf16[384,4096]{0,1:T(8,128)(2,1)} %all-gather.11.cloned.1.call-done) | copy-start | bytes 9437188
  408.6 65.3 %copy-start = (f32[384,16,128]{2,0,1:T(8,128)}, f32[384,16,128]{2,0,1:T(8,128)S(1)}, u32[]{:S(2)}) copy-start(f32[384,16,128]{2,0,1:T(8,128)S(1)} %scatter_fusion) | copy-start | bytes 9437188
  523.0 9.5 copy-start.1
  540.4 9.5 copy-start.1
  557.7 9.5 copy-start.1
  575.1 9.5 copy-start.1
  609.9 9.5 copy-start.1
  627.2 9.5 copy-start.1
  662.0 9.5 copy-start.1
  696.8 9.5 copy-start.1
  714.2 9.5 copy-start.1
  731.6 9.5 copy-start.1
  749.0 9.5 copy-start.1
  813.5 355.3 %reduce-scatter.8.cloned.1.call-start = ((), (), s32[]{:S(2)}) async-start(), calls=%async_computation.8 | async-start | bytes 3538944 | tf_op jit(solution)/shard_map/reduce_scatter | solution.py:88
  853.2 390.1 %reduce-scatter.6.cloned.1.call-start = ((), (), s32[]{:S(2)}) async-start(), calls=%async_computation.6 | async-start | bytes 3538944 | tf_op jit(solution)/shard_map/reduce_scatter | solution.py:56
  (45 other events, 326.0 us)
Sparse Core Ops, SparseCore 0:
  10.2 72.9 all-gather.10
  85.6 56.7 all-gather.8
  144.9 54.6 all-gather.12
  201.7 69.5 all-gather.16
  273.5 56.3 all-gather.14
  813.7 277.8 all-reduce.2
  1094.6 74.1 reduce-scatter.7
  1171.8 71.5 reduce-scatter.5
where the time goes:
time: 1260 us; the launch traced here: 1250 us
  waiting for transfers between devices  532 us (42%)
  local copies, waits for them, and re-layouts  302 us (24%)
  other arithmetic  167 us (13%)
  matrix products  150 us (12%)
  blocking collectives  71.7 us (6%)
  between operations  15.1 us (1%)
    unnamed x9, waiting for transfers between devices  219 us
    scatter-add x3, other arithmetic, spread_columns(): return empty.at[:, columns.reshape(-1)].add(flat)  140 us
    gather x32, local copies, waits for them, and re-layouts, one_group(): jnp.take(up_delta, up_local, axis=1)  86.3 us
    reduce_scatter x1, waiting for transfers between devices, body(): lax.psum_scatter(partial_value.reshape(tok_rows, -1).astype(jnp.bfloat16)...  75.2 us
    reduce_scatter x1, waiting for transfers between devices, body(): lax.psum_scatter(out_acc.reshape(tok_rows, -1).astype(jnp.bfloat16), 'col...  74.5 us
    reshape x3, local copies, waits for them, and re-layouts, spread_columns(): flat = products.reshape(tok_rows, -1, products.shape[3])  74.5 us
    all_gather x1, waiting for transfers between devices, body(): down_vals = lax.all_gather(down_blocks, 'row', axis=0, tiled=True)  58.6 us
    all_gather x1, waiting for transfers between devices, body(): gate_vals = lax.all_gather(gate_blocks, 'row', axis=0, tiled=True)  55 us
  transfers between devices with their start and end apart: 8, of which 7 were waited for; matrix products, arithmetic and copies ran while one was open for 12% of the time, Pallas kernels for 0%

commit v1 on v0

--- a/solution.py
+++ b/solution.py
@@ -1,7 +1,20 @@
+import functools
 import jax
 import jax.numpy as jnp
 from jax import lax
 from jax.sharding import PartitionSpec as P
+from jax.lax import all_to_all, axis_size
+
+
+def choose_arrays(packet, which_axis, array_dim):
+    prior = axis_size(which_axis)
+    ready = jnp.stack([packet] * prior, axis=0)
+    block_next = all_to_all(ready, axis_name=which_axis, split_axis=0, concat_axis=0)
+    all_rows = jnp.concatenate(block_next, axis=array_dim)
+    return all_rows
+
+
+_note_cards = functools.partial(choose_arrays, which_axis="row", array_dim=0)
 
 
 def spread_columns(products, columns, local_width):
@@ -43,7 +56,7 @@
     gate_acc, up_acc, gate_idx, up_idx = (gate_acc, up_acc, gate_gate_idx, gate_up_idx)
     silu_gate = jax.nn.silu(gate_acc)
     hidden_blocks = (silu_gate * up_acc).astype(jnp.bfloat16)
-    down_vals = lax.all_gather(down_blocks, "row", axis=0, tiled=True)
+    down_vals = _note_cards(down_blocks)
     down_piece = lax.all_gather(down_cols.astype(jnp.bfloat16), "row", axis=0, tiled=True)
     down_local = down_piece.astype(jnp.int32) - offset
     chosen = jnp.take(hidden_blocks, down_local, axis=1)

time: 1260 us -> 1300 us (1.032)
  waiting for transfers between devices: 532 us -> 570 us
    all_to_all x0 -> x1, waiting for transfers between devices: none -> 54.1 us  [choose_arrays(): all_to_all(ready, axis_name=which_axis, split_axis=0, concat_axis=0)]
    unnamed x9, waiting for transfers between devices: 219 us -> 203 us
  transfers between devices with their start and end apart: 8 -> 9, of which waited for: 7 -> 8; matrix products, arithmetic and copies ran while one was open for 12% -> 11% of each run, Pallas kernels for 0% -> 0%
where the time goes in v1:
time: 1300 us
  waiting for transfers between devices  570 us (44%)
  local copies, waits for them, and re-layouts  303 us (23%)
  other arithmetic  167 us (13%)
  matrix products  152 us (12%)
  blocking collectives  71.7 us (6%)
  between operations  15.1 us (1%)
    unnamed x9, waiting for transfers between devices  203 us
    scatter-add x3, other arithmetic, spread_columns(): return empty.at[:, columns.reshape(-1)].add(flat)  141 us
    gather x32, local copies, waits for them, and re-layouts, one_group(): jnp.take(up_delta, up_local, axis=1)  86.5 us
    reduce_scatter x1, waiting for transfers between devices, body(): lax.psum_scatter(partial_value.reshape(tok_rows, -1).astype(jnp.bfloat16)...  75.2 us
    reduce_scatter x1, waiting for transfers between devices, body(): lax.psum_scatter(out_acc.reshape(tok_rows, -1).astype(jnp.bfloat16), 'col...  74.5 us
    reshape x3, local copies, waits for them, and re-layouts, spread_columns(): flat = products.reshape(tok_rows, -1, products.shape[3])  74.5 us
    all_gather x1, waiting for transfers between devices, body(): lax.all_gather(down_blocks, 'row', axis=0, tiled=True)  58.6 us
    all_gather x1, waiting for transfers between devices, body(): gate_vals = lax.all_gather(gate_blocks, 'row', axis=0, tiled=True)  55 us
  transfers between devices with their start and end apart: 9, of which 8 were waited for; matrix products, arithmetic and copies ran while one was open for 11% of the time, Pallas kernels for 0%

profile of v1, /device:TPU:2, one launch (start us, length us, event | category | flops | bytes accessed | tf_op | source)
XLA Modules:
  0.0 1296.0 jit_solution(18024815520208544493)
XLA Ops:
  14.0 28.0 %all-gather = bf16[16,2,4]{2,1,0:T(2,128)(2,1)S(1)} all-gather(bf16[1,2,4]{2,1,0:T(2,128)(2,1)S(1)} %convert_bitcast_fusion.2), channel_id=1, replica_groups=mesh['row'=16,'col'=8] {'row'}, dimensions={0}, use_global_device_ids=true | all-gather | bytes 272 | tf_op jit(solution)/shard_map/all_gather | solution.py:43
  42.8 19.2 %all-gather.1 = bf16[16,2,4]{2,1,0:T(2,128)(2,1)S(1)} all-gather(bf16[1,2,4]{2,1,0:T(2,128)(2,1)S(1)} %convert_bitcast_fusion.1), channel_id=1, replica_groups=mesh['row'=16,'col'=8] {'row'}, dimensions={0}, use_global_device_ids=true | all-gather | bytes 272 | tf_op jit(solution)/shard_map/all_gather | solution.py:44
  62.8 24.5 %all-gather.2 = bf16[16,2,4]{2,1,0:T(2,128)(2,1)S(1)} all-gather(bf16[1,2,4]{2,1,0:T(2,128)(2,1)S(1)} %convert_bitcast_fusion), channel_id=1, replica_groups=mesh['row'=16,'col'=8] {'row'}, dimensions={0}, use_global_device_ids=true | all-gather | bytes 272 | tf_op jit(solution)/shard_map/all_gather | solution.py:60
  87.4 55.0 %all-gather.9.cloned.1.call-done = bf16[32,4,128,128]{3,2,1,0:T(8,128)(2,1)} async-done(((bf16[2,4,128,128]{3,2,1,0:T(8,128)(2,1)}), bf16[32,4,128,128]{3,2,1,0:T(8,128)(2,1)}) %all-gather.9.cloned.1.call-update) | async-done | bytes 4194320 | tf_op jit(solution)/shard_map/all_gather | solution.py:41
  142.5 15.2 %fusion.52 = f32[32,4,128,384]{3,2,1,0:T(8,128)} fusion(bf16[32,4,128,128]{3,2,1,0:T(8,128)(2,1)} %all-gather.9.cloned.1.call-done, bf16[384,32,128,1]{0,2,3,1:T(8,128)(2,1)} %bitcast.177), kind=kOutput, calls=%fused_computation.100 | convolution fusion | flops 1610612736 | bytes 32505856 | tf_op jit(solution)/shard_map/tkd,kjde->tkje/dot_general | solution.py:48
  157.7 25.0 %copy.57 = f32[384,128,128]{2,0,1:T(8,128)} copy(f32[384,128,128]{0,2,1:T(8,128)} %bitcast.168) | data formatting | bytes 50331648 | tf_op jit(solution)/shard_map/reshape | solution.py:22
  182.7 16.9 %all-gather.13.cloned.1.call-done = bf16[32,4,128,128]{3,2,1,0:T(8,128)(2,1)} async-done(((bf16[2,4,128,128]{3,2,1,0:T(8,128)(2,1)}), bf16[32,4,128,128]{3,2,1,0:T(8,128)(2,1)}) %all-gather.13.cloned.1.call-update) | async-done | bytes 4194320 | tf_op jit(solution)/shard_map/all_gather | solution.py:42
  199.6 14.1 %fusion.53 = f32[32,4,128,384]{3,2,1,0:T(8,128)} fusion(bf16[32,4,128,128]{3,2,1,0:T(8,128)(2,1)} %all-gather.13.cloned.1.call-done, bf16[384,32,128,1]{0,2,3,1:T(8,128)(2,1)S(1)} %bitcast.179), kind=kOutput, calls=%fused_computation.101 | convolution fusion | flops 1610612736 | bytes 32505856 | tf_op jit(solution)/shard_map/tkd,kjde->tkje/dot_general | solution.py:51
  213.7 24.8 %copy.60 = f32[384,128,128]{2,0,1:T(8,128)} copy(f32[384,128,128]{0,2,1:T(8,128)} %bitcast.169) | data formatting | bytes 50331648 | tf_op jit(solution)/shard_map/reshape | solution.py:22
  238.5 32.8 %all-gather.17.cloned.1.call-done = bf16[384,4096]{0,1:T(8,128)(2,1)} async-done(((bf16[384,512]{0,1:T(8,128)(2,1)}), bf16[384,4096]{0,1:T(8,128)(2,1)}) %all-gather.17.cloned.1.call-update) | async-done | bytes 3145744 | tf_op jit(solution)/shard_map/all_gather | solution.py:36
  271.3 58.6 %all-gather.15.cloned.1.call-done = bf16[32,4,128,128]{3,2,1,0:T(8,128)(2,1)} async-done(((bf16[2,4,128,128]{3,2,1,0:T(8,128)(2,1)}), bf16[32,4,128,128]{3,2,1,0:T(8,128)(2,1)}) %all-gather.15.cloned.1.call-update) | async-done | bytes 4194320 | tf_op jit(solution)/shard_map/all_gather | solution.py:76
  329.9 15.0 %fusion.54 = f32[32,4,128,384]{3,2,1,0:T(8,128)} fusion(bf16[32,4,128,128]{3,2,1,0:T(8,128)(2,1)} %all-gather.15.cloned.1.call-done, bf16[384,32,128,1]{0,2,3,1:T(8,128)(2,1)} %bitcast.183), kind=kOutput, calls=%fused_computation.102 | convolution fusion | flops 1610612736 | bytes 32505856 | tf_op jit(solution)/shard_map/tkd,kjde->tkje/dot_general | solution.py:73
  344.9 24.7 %copy.65 = f32[384,128,128]{2,0,1:T(8,128)} copy(f32[384,128,128]{0,2,1:T(8,128)} %bitcast.167) | data formatting | bytes 50331648 | tf_op jit(solution)/shard_map/reshape | solution.py:22
  369.9 38.7 %scatter_fusion = f32[384,16,128]{2,0,1:T(8,128)S(1)} fusion(f32[384,16,128]{2,0,1:T(8,128)S(1)} %broadcast.82.clone, s32[128]{0:T(128)S(1)} %fusion.46, f32[128,384,128]{2,1,0:T(8,128)} %bitcast.170), kind=kCustom, calls=%fused_computation.6 | custom fusion | flops 6291456 | bytes 75497984 | tf_op jit(solution)/shard_map/scatter-add | solution.py:24
  410.8 63.2 %scatter_fusion.1 = f32[384,16,128]{2,0,1:T(8,128)} fusion(f32[384,16,128]{2,0,1:T(8,128)} %broadcast.82.clone.2, s32[128]{0:T(128)S(1)} %fusion.47, f32[128,384,128]{2,1,0:T(8,128)} %bitcast.171), kind=kCustom, calls=%fused_computation.7 | custom fusion | flops 6291456 | bytes 75497984 | tf_op jit(solution)/shard_map/scatter-add | solution.py:24
  474.3 38.7 %scatter_fusion.2 = f32[384,16,128]{2,0,1:T(8,128)S(1)} fusion(f32[384,16,128]{2,0,1:T(8,128)S(1)} %broadcast.82.clone.1, s32[128]{0:T(128)S(1)} %fusion.48, f32[128,384,128]{2,1,0:T(8,128)} %bitcast.172), kind=kCustom, calls=%fused_computation.8 | custom fusion | flops 6291456 | bytes 75497984 | tf_op jit(solution)/shard_map/scatter-add | solution.py:24
  518.8 278.3 %while.10 = (s32[]{:T(128)}, bf16[16,2,3,4,128,128]{4,5,3,1,2,0:T(8,128)(2,1)}, s32[16]{0:T(128)S(1)}, s32[32,4]{1,0:T(8,128)S(1)}, bf16[384,16,128]{2,0,1:T(8,1...) while((s32[]{:T(128)}, ...), condition=%wide.region_6.9_spmd, body=%wide.region_5.8_spmd.sunk | while | flops 304352384 | bytes 31798688 | solution.py:137
  797.1 16.6 %copy.69 = bf16[16,2,3,4,128,128]{5,4,3,1,0,2:T(8,128)(2,1)} copy(bf16[16,2,3,4,128,128]{4,5,3,1,2,0:T(8,128)(2,1)} %get-tuple-element.64) | data formatting | bytes 25165824 | tf_op jit(solution)/shard_map/convert_element_type | solution.py:139
  832.3 9.7 fusion.25
  842.1 8.8 fusion.37
  870.4 54.1 %all-to-all-done = bf16[16,2,4,128,128]{4,3,2,1,0:T(8,128)(2,1)} async-done(((bf16[16,2,4,128,128]{4,3,2,1,0:T(8,128)(2,1)}), bf16[16,2,4,128,128]{4,3,2,1,0:T(8,128)(2,1)}, u32[]{:S(2)}, u32[]{:S(2)}) %all-to-all-start) | async-done | bytes 4194336 | tf_op jit(solution)/shard_map/all_to_all | solution.py:12
  936.8 200.6 %all-reduce.3.cloned.1.call-done = bf16[32,3,4,128,128]{4,3,2,0,1:T(8,128)(2,1)} async-done(((bf16[32,3,4,128,128]{4,3,2,0,1:T(8,128)(2,1)}), bf16[32,3,4,128,128]{4,3,2,0,1:T(8,128)(2,1)}) %all-reduce.3.cloned.1.call-update) | async-done | bytes 12582928
  1139.4 75.2 %reduce-scatter.8.cloned.1.call-done = bf16[384,512]{1,0:T(8,128)(2,1)} async-done(((bf16[384,4096]{1,0:T(8,128)(2,1)}), bf16[384,512]{1,0:T(8,128)(2,1)}) %reduce-scatter.8.cloned.1.call-update) | async-done | bytes 393232 | tf_op jit(solution)/shard_map/reduce_scatter | solution.py:101
  1214.6 74.5 %reduce-scatter.6.cloned.1.call-done = bf16[384,512]{1,0:T(8,128)(2,1)} async-done(((bf16[384,4096]{1,0:T(8,128)(2,1)}), bf16[384,512]{1,0:T(8,128)(2,1)}) %reduce-scatter.6.cloned.1.call-update) | async-done | bytes 393232 | tf_op jit(solution)/shard_map/reduce_scatter | solution.py:69
  (487 shorter events, 335.5 us)
Async XLA Ops:
  7.2 80.3 %all-gather.11.cloned.1.call-start = ((), (), s32[]{:S(2)}) async-start(), calls=%async_computation.4 | async-start | bytes 3538944 | tf_op jit(solution)/shard_map/all_gather | solution.py:35
  9.1 133.3 %all-gather.9.cloned.1.call-start = ((), (), s32[]{:S(2)}) async-start(), calls=%async_computation.3 | async-start | bytes 4456448 | tf_op jit(solution)/shard_map/all_gather | solution.py:41
  9.9 189.7 %all-gather.13.cloned.1.call-start = ((), (), s32[]{:S(2)}) async-start(), calls=%async_computation.5 | async-start | bytes 4456448 | tf_op jit(solution)/shard_map/all_gather | solution.py:42
  10.6 260.7 %all-gather.17.cloned.1.call-start = ((), (), s32[]{:S(2)}) async-start(), calls=%async_computation.8 | async-start | bytes 3538944 | tf_op jit(solution)/shard_map/all_gather | solution.py:36
  12.6 317.3 %all-gather.15.cloned.1.call-start = ((), (), s32[]{:S(2)}) async-start(), calls=%async_computation.7 | async-start | bytes 4456448 | tf_op jit(solution)/shard_map/all_gather | solution.py:76
  13.2 1124.2 %all-reduce.3.cloned.1.call-start = ((), (), s32[]{:S(2)}) async-start(), calls=%async_computation.10 | async-start | bytes 25165824
  42.0 45.3 %copy-start.12 = (s32[4,8,4]{2,1,0:T(8,128)}, s32[4,8,4]{2,1,0:T(8,128)S(1)}, u32[]{:S(2)}) copy-start(s32[4,8,4]{2,1,0:T(8,128)S(1)} %convert_subtract_fusion.2) | copy-start | bytes 1540
  62.0 95.7 %copy-start.14 = (s32[4,8,4]{2,1,0:T(8,128)}, s32[4,8,4]{2,1,0:T(8,128)S(1)}, u32[]{:S(2)}) copy-start(s32[4,8,4]{2,1,0:T(8,128)S(1)} %convert_subtract_fusion.1) | copy-start | bytes 1540
  87.2 70.4 %copy-start.10 = (s32[4,8,4]{2,1,0:T(8,128)}, s32[4,8,4]{2,1,0:T(8,128)S(1)}, u32[]{:S(2)}) copy-start(s32[4,8,4]{2,1,0:T(8,128)S(1)} %convert_subtract_fusion) | copy-start | bytes 1540
  157.7 41.9 %copy-start.6 = (bf16[384,4096]{0,1:T(8,128)(2,1)S(1)}, bf16[384,4096]{0,1:T(8,128)(2,1)}, u32[]{:S(2)}) copy-start(bf16[384,4096]{0,1:T(8,128)(2,1)} %all-gather.11.cloned.1.call-done) | copy-start | bytes 9437188
  408.6 65.5 %copy-start = (f32[384,16,128]{2,0,1:T(8,128)}, f32[384,16,128]{2,0,1:T(8,128)S(1)}, u32[]{:S(2)}) copy-start(f32[384,16,128]{2,0,1:T(8,128)S(1)} %scatter_fusion) | copy-start | bytes 9437188
  523.1 9.5 copy-start.1
  540.5 9.5 copy-start.1
  557.9 9.5 copy-start.1
  679.6 9.5 copy-start.1
  697.0 9.5 copy-start.1
  714.4 9.5 copy-start.1
  731.8 9.5 copy-start.1
  749.2 9.5 copy-start.1
  766.7 9.5 copy-start.1
  813.8 400.8 %reduce-scatter.8.cloned.1.call-start = ((), (), s32[]{:S(2)}) async-start(), calls=%async_computation.9 | async-start | bytes 3538944 | tf_op jit(solution)/shard_map/reduce_scatter | solution.py:101
  832.3 9.7 copy-start.7
  857.0 67.5 %all-to-all-start = ((bf16[16,2,4,128,128]{4,3,2,1,0:T(8,128)(2,1)}), bf16[16,2,4,128,128]{4,3,2,1,0:T(8,128)(2,1)}, u32[]{:S(2)}, u32[]{:S(2)}) async-start(bf16[16,2,4,128,128]{4,3,2,1,0:T(8,128)(2,1)} %stack.10), calls=%async_computation | async-start | bytes 8388608 | tf_op jit(solution)/shard_map/all_to_all | solution.py:12
  861.7 427.5 %reduce-scatter.6.cloned.1.call-start = ((), (), s32[]{:S(2)}) async-start(), calls=%async_computation.6 | async-start | bytes 3538944 | tf_op jit(solution)/shard_map/reduce_scatter | solution.py:69
  (47 other events, 339.9 us)
Sparse Core Ops, SparseCore 0:
  10.2 72.9 all-gather.10
  85.6 56.7 all-gather.8
  144.9 54.6 all-gather.12
  201.7 69.5 all-gather.16
  273.5 56.3 all-gather.14
  813.9 323.4 all-reduce.2
  1140.4 74.1 reduce-scatter.7
  1217.6 71.5 reduce-scatter.5
